TPU v7x, 128 devices: a whole 4x4x4 slice. The times are simulated.
128 devices in a mesh: rack: 64 (over y, z, x_hi, core), queue: 2 (over x_lo).
Axes of the slice: x: 4 (x_hi: 2, x_lo: 2; x = x_hi * 2 + x_lo), y: 4, z: 4, core: 2. Of those that a mesh axis runs over, the one named last changes fastest.
Arguments:
- state: float32 [4096, 4096], P('rack', 'queue'), may hold values from -6 to 6
- queue_blocks: float32 [16, 3, 256, 256], P('queue'), may hold values from -0.21875 to 0.21875
- queue_rows: int32 [16, 3], P('queue'), may hold values from 0 to 15, as said below
- kill_blocks: float32 [16, 3, 256, 256], P('queue'), may hold values from -0.21875 to 0.21875
- kill_rows: int32 [16, 3], P('queue'), may hold values from 0 to 15, as said below
- rate_index: int32 [12], replicated, may hold values from 0 to 7
- rate_table: float32 [8, 2], replicated, may hold values from 0.1 to 2
Outputs:
- advanced: float32 [4096, 4096], P('rack', 'queue')
Inputs may be any that keep to these rules, and one draw needn't show every extreme that they name: `queue_rows`: column block c's first row block is c, and its three row blocks are distinct. `kill_rows`: column block c's first row block is c, and its three row blocks are distinct.
All inputs are finite; a program needn't handle non-finite values.
Results may differ from a plain program's by a relative error of at most 0.0001.
Values sent between devices are 32-bit elements; how exact they have to be, the bound alone decides.
A program may use at most 128 MiB of HBM per device.

v0:
```python
import jax
import jax.numpy as jnp
from jax import lax
from jax.sharding import PartitionSpec as P

STEPS = 2


def from_partner(value, axis, stride):
    mask = 2**stride
    pairs = [(source, source ^ mask) for source in range(lax.axis_size(axis))]
    return lax.ppermute(value, axis, pairs)


def apply_blocks(whole, blocks, rows):
    patterns = whole.shape[0]
    pieces = whole.reshape(patterns, -1, blocks.shape[2])
    chosen = jnp.take(pieces, rows, axis=1)
    result = jnp.einsum(
        "pcjt,cjts->pcs",
        chosen,
        blocks,
        precision=lax.Precision.HIGHEST,
        preferred_element_type=jnp.float32,
    )
    return result.reshape(patterns, -1)


def bit_terms(current, killed, fail, repair, first, count):
    total = jnp.zeros_like(current)
    rows = current.shape[0]
    for bit in range(count):
        shape = (rows // 2 ** (bit + 1), 2, 2**bit) + current.shape[1:]
        upper = current.reshape(shape)
        lower = killed.reshape(shape)
        term = jnp.stack(
            (repair[first + bit] * upper[:, 1], fail[first + bit] * lower[:, 0]), axis=1
        )
        total = total + term.reshape(current.shape)
    return total


def local(state, queue_blocks, queue_rows, kill_blocks, kill_rows, rate_index, rate_table):
    fail = rate_table[rate_index, 0]
    repair = rate_table[rate_index, 1]
    scale_sum = 1.0 + jnp.sum(fail + repair)
    patterns = state.shape[0]
    low_count = patterns.bit_length() - 1
    high_count = lax.axis_size("rack").bit_length() - 1
    rack_place = lax.axis_index("rack")
    pattern = lax.broadcasted_iota(jnp.int32, (patterns, 1), 0)
    leaving = jnp.zeros((patterns, 1), jnp.float32)
    for bit in range(low_count):
        flag = pattern // 2**bit % 2
        leaving = leaving + jnp.where(flag == 1, repair[bit], fail[bit])
    for bit in range(high_count):
        flag = rack_place // 2**bit % 2
        leaving = leaving + jnp.where(flag == 1, repair[low_count + bit], fail[low_count + bit])
    current = state
    for step in range(STEPS):
        whole = lax.all_gather(current, "queue", axis=1, tiled=True)
        queue_part = apply_blocks(whole, queue_blocks, queue_rows)
        killed = apply_blocks(whole, kill_blocks, kill_rows)
        rack_part = bit_terms(current, killed, fail, repair, 0, low_count)
        order = range(high_count)
        for bit in order:
            flag = rack_place // 2**bit % 2
            outgoing = jnp.where(flag == 1, current, killed)
            incoming = from_partner(outgoing, "rack", bit)
            rack_part = (
                rack_part
                + jnp.where(flag == 1, fail[low_count + bit], repair[low_count + bit]) * incoming
            )
        current = current + (queue_part + rack_part - leaving * current) / scale_sum
    return current


def solution(mesh):
    placed = (
        P("rack", "queue"),
        P("queue", None, None, None),
        P("queue", None),
        P("queue", None, None, None),
        P("queue", None),
        P(),
        P(),
    )
    return jax.shard_map(
        local, mesh=mesh, in_specs=placed, out_specs=P("rack", "queue"), check_vma=False
    )
```

profile of v0, /device:TPU:68, one launch (start us, length us, event | category | flops | bytes accessed | tf_op | source)
XLA Modules:
  0.0 195.9 jit_solution(13551869775011367674)
XLA Ops:
  27.2 7.4 %add_add_fusion = f32[64]{0:T(128)S(1)} fusion(f32[]{:T(128)S(6)} %select_n.398, f32[]{:T(128)S(6)} %select_n.397, f32[]{:T(128)S(6)} %select_n.396, f32[]{:T(128)S(6)} %select_n.395, f32[]{:T(128)S(6)} %select_n.394, f32[]{:T(128)S(6)} %select_n.393, f32[]{:T(128)} %bitcast.27, f32[]{:T(128)} %bitcast.25, f32[]{:T(128)} %bitcast.23, f32[]{:T(128)} %bitcast.21, ...), kind=kLoop, calls=%fused_computation.162 | loop fusion | flops 7296 | bytes 328 | tf_op jit(solution)/shard_map/add | solution.py:58
  48.1 1.8 gather_fusion.3
  49.9 7.3 %fusion.4 = f32[8,64,256,1]{2,1,3,0:T(8,128)S(1)} fusion(f32[8,3,256,256]{3,2,1,0:T(8,128)} %param.12, f32[8,3,64,256]{3,2,1,0:T(8,128)} %bitcast.165, pred[8,3]{1,0:T(8,128)(4,1)S(1)} %copy.48), kind=kOutput, calls=%fused_computation.10 | convolution fusion | flops 1208352768 | bytes 8388632 | tf_op jit(solution)/shard_map/pcjt,cjts->pcs/dot_general | solution.py:19
  61.5 1.8 gather_fusion.2
  65.0 2.3 %slice_multiply_fusion.14 = f32[2,1,16,2048]{3,2,1,0:T(8,128)} fusion(f32[2,2,16,2048]{3,2,1,0:T(8,128)} %reshape_reshape.40, f32[]{:T(128)} %bitcast.23), kind=kLoop, calls=%fused_computation.82 | loop fusion | flops 65536 | bytes 524292 | tf_op jit(solution)/shard_map/mul | solution.py:37
  67.3 2.4 %slice_multiply_fusion.16 = f32[4,1,8,2048]{3,2,1,0:T(8,128)} fusion(f32[4,2,8,2048]{3,2,1,0:T(8,128)} %reshape_reshape.39, f32[]{:T(128)} %bitcast.19), kind=kLoop, calls=%fused_computation.84 | loop fusion | flops 65536 | bytes 524292 | tf_op jit(solution)/shard_map/mul | solution.py:37
  71.5 3.2 %collective-permute-start.5 = (f32[64,2048]{1,0:T(8,128)}, f32[64,2048]{1,0:T(8,128)}, u32[]{:S(2)}, u32[]{:S(2)}) collective-permute-start(f32[64,2048]{1,0:T(8,128)} %get-tuple-element.19), channel_id=1, source_target_pairs={{0,64},{2,66},{4,68},{6,70},{8,72},{10,74},{12,76},{14,78},{16,80}... | collective-permute-start | bytes 1572872 | tf_op jit(solution)/shard_map/ppermute | solution.py:12
  75.4 2.2 %collective-permute-start.2 = (f32[64,2048]{1,0:T(8,128)}, f32[64,2048]{1,0:T(8,128)}, u32[]{:S(2)}, u32[]{:S(2)}) collective-permute-start(f32[64,2048]{1,0:T(8,128)} %get-tuple-element.17), channel_id=1, source_target_pairs={{0,8},{2,10},{4,12},{6,14},{8,0},{10,2},{12,4},{14,6},{16,24},{18,... | collective-permute-start | bytes 1572872 | tf_op jit(solution)/shard_map/ppermute | solution.py:12
  79.8 6.2 %fusion.12 = f32[8,8,8,256]{3,2,1,0:T(8,128)S(1)} fusion(f32[8,3,256,256]{3,2,1,0:T(8,128)} %param.10, f32[8,3,64,256]{3,2,1,0:T(8,128)S(1)} %bitcast.162, pred[8,3]{1,0:T(8,128)(4,1)S(1)} %copy.44), kind=kOutput, calls=%fused_computation.18 | convolution fusion | flops 1208352768 | bytes 8388632 | tf_op jit(solution)/shard_map/pcjt,cjts->pcs/dot_general | solution.py:19
  89.4 2.1 %pad_maximum_fusion.1 = f32[16,2,2,2048]{3,2,1,0:T(2,128)} fusion(f32[16,1,2,2048]{3,2,1,0:T(2,128)S(1)} %slice_multiply_fusion.20, f32[16,1,2,2048]{3,2,1,0:T(2,128)} %slice_multiply_fusion.21), kind=kLoop, calls=%fused_computation.31 | loop fusion | flops 131072 | bytes 1048576 | tf_op jit(solution)/shard_map/stack | solution.py:36
  95.6 3.0 %collective-permute-done.4 = f32[64,2048]{1,0:T(8,128)} collective-permute-done((f32[64,2048]{1,0:T(8,128)}, f32[64,2048]{1,0:T(8,128)}, u32[]{:S(2)}, u32[]{:S(2)}) %collective-permute-start.4) | collective-permute-done | bytes 524320 | tf_op jit(solution)/shard_map/ppermute | solution.py:12
  100.2 3.4 %fusion.45 = f32[64,2048]{1,0:T(8,128)} fusion(f32[64,2048]{1,0:T(8,128)S(1)} %copy-done.3, f32[64,2048]{1,0:T(8,128)S(1)} %bitcast.171, f32[1,2,32,2048]{3,2,1,0:T(8,128)S(1)} %pad_maximum_fusion.5, f32[2,2,16,2048]{3,2,1,0:T(8,128)S(1)} %pad_maximum_fusion.4, f32[4,2,8,2048]{3,2,1,0:T(8,128)S(1)} %pad_maximum_fusion.3, ...), kind=kLoop, calls=%fused_computation.65 | loop fusion | flops 2883584 | bytes 7864604 | tf_op jit(solution)/shard_map/add | solution.py:74
  113.2 14.2 %all-gather.5.cloned.1.call-done = f32[64,4096]{1,0:T(8,128)} async-done(((f32[64,2048]{1,0:T(8,128)}), f32[64,4096]{1,0:T(8,128)}) %all-gather.5.cloned.1.call-update) | async-done | bytes 1048592 | tf_op jit(solution)/shard_map/all_gather | solution.py:61
  129.4 1.8 gather_fusion.5
  131.2 7.3 %fusion = f32[8,64,256,1]{2,1,3,0:T(8,128)S(1)} fusion(f32[8,3,256,256]{3,2,1,0:T(8,128)} %param.12, f32[8,3,64,256]{3,2,1,0:T(8,128)} %bitcast.164, pred[8,3]{1,0:T(8,128)(4,1)S(1)} %copy.48), kind=kOutput, calls=%fused_computation.6 | convolution fusion | flops 1208352768 | bytes 8388632 | tf_op jit(solution)/shard_map/pcjt,cjts->pcs/dot_general | solution.py:19
  143.7 7.7 %fusion.15 = f32[8,8,8,256]{3,2,1,0:T(8,128)} fusion(f32[8,3,256,256]{3,2,1,0:T(8,128)} %param.10, f32[8,3,64,256]{3,2,1,0:T(8,128)S(1)} %bitcast.163, pred[8,3]{1,0:T(8,128)(4,1)S(1)} %copy.44), kind=kOutput, calls=%fused_computation.19 | convolution fusion | flops 1208352768 | bytes 8388632 | tf_op jit(solution)/shard_map/pcjt,cjts->pcs/dot_general | solution.py:19
  154.9 2.0 %broadcast_select_fusion.10 = (f32[64,2048]{1,0:T(8,128)}, f32[64,2048]{1,0:T(8,128)}, f32[64,2048]{1,0:T(8,128)}, f32[64,2048]{1,0:T(8,128)}, f32[64,2048]{1,0:T(8,128)}, /*index=5*/f32[64,2048]{1,0:T(8,128)}) fusion(f32[64,2048]{1,0:T(8,128)S(1)} %copy-done.2, f32[64,2048]{1,0:T(8,128)S(1)} %bitcast.172, pred[]{:T(512)S(6)} %eq.116, pred[]{:T(512)S(6)} %eq.121, ...), kind=kLoop, calls=%fused_computation.102 | loop fusion | flops 786432 | bytes 4194310 | tf_op jit(solution)/shard_map/jit(_where)/select_n | solution.py:68
  156.9 3.0 %collective-permute-start.11 = (f32[64,2048]{1,0:T(8,128)}, f32[64,2048]{1,0:T(8,128)}, u32[]{:S(2)}, u32[]{:S(2)}) collective-permute-start(f32[64,2048]{1,0:T(8,128)} %get-tuple-element.9), channel_id=1, source_target_pairs={{0,64},{2,66},{4,68},{6,70},{8,72},{10,74},{12,76},{14,78},{16,80}... | collective-permute-start | bytes 1572872 | tf_op jit(solution)/shard_map/ppermute | solution.py:12
  160.9 2.2 %collective-permute-start.8 = (f32[64,2048]{1,0:T(8,128)}, f32[64,2048]{1,0:T(8,128)}, u32[]{:S(2)}, u32[]{:S(2)}) collective-permute-start(f32[64,2048]{1,0:T(8,128)} %get-tuple-element.12), channel_id=1, source_target_pairs={{0,8},{2,10},{4,12},{6,14},{8,0},{10,2},{12,4},{14,6},{16,24},{18,... | collective-permute-start | bytes 1572872 | tf_op jit(solution)/shard_map/ppermute | solution.py:12
  168.9 4.6 %collective-permute-done.11 = f32[64,2048]{1,0:T(8,128)} collective-permute-done((f32[64,2048]{1,0:T(8,128)}, f32[64,2048]{1,0:T(8,128)}, u32[]{:S(2)}, u32[]{:S(2)}) %collective-permute-start.11) | collective-permute-done | bytes 524320 | tf_op jit(solution)/shard_map/ppermute | solution.py:12
  173.6 2.1 %pad_maximum_fusion.7 = f32[16,2,2,2048]{3,2,1,0:T(2,128)} fusion(f32[16,1,2,2048]{3,2,1,0:T(2,128)S(1)} %slice_multiply_fusion.8, f32[16,1,2,2048]{3,2,1,0:T(2,128)} %slice_multiply_fusion.9), kind=kLoop, calls=%fused_computation.37 | loop fusion | flops 131072 | bytes 1048576 | tf_op jit(solution)/shard_map/stack | solution.py:36
  179.8 3.9 %collective-permute-done.10 = f32[64,2048]{1,0:T(8,128)} collective-permute-done((f32[64,2048]{1,0:T(8,128)}, f32[64,2048]{1,0:T(8,128)}, u32[]{:S(2)}, u32[]{:S(2)}) %collective-permute-start.10) | collective-permute-done | bytes 524320 | tf_op jit(solution)/shard_map/ppermute | solution.py:12
  183.7 1.9 collective-permute-done.8
  185.7 3.4 %fusion.35 = f32[64,2048]{1,0:T(8,128)} fusion(f32[64,2048]{1,0:T(8,128)S(1)} %copy-done.2, f32[64,2048]{1,0:T(8,128)S(1)} %bitcast.170, f32[1,2,32,2048]{3,2,1,0:T(8,128)S(1)} %pad_maximum_fusion.11, f32[2,2,16,2048]{3,2,1,0:T(8,128)S(1)} %pad_maximum_fusion.10, f32[4,2,8,2048]{3,2,1,0:T(8,128)S(1)} %pad_maximum_fusion.9, ...), kind=kLoop, calls=%fused_computation.52 | loop fusion | flops 2883584 | bytes 7864604 | tf_op jit(solution)/shard_map/add | solution.py:74
  (143 shorter events, 69.0 us)
Async XLA Ops:
  6.5 8.5 %copy-start.3 = (f32[64,2048]{1,0:T(8,128)S(1)}, f32[64,2048]{1,0:T(8,128)}, u32[]{:S(2)}) copy-start(f32[64,2048]{1,0:T(8,128)} %param.9) | copy-start | bytes 1572868
  6.5 40.2 %all-gather.3.cloned.1.call-start = ((), (), s32[]{:S(2)}) async-start(), calls=%async_computation | async-start | bytes 1572864 | tf_op jit(solution)/shard_map/all_gather | solution.py:61
  7.3 120.1 %all-gather.5.cloned.1.call-start = ((), (), s32[]{:S(2)}) async-start(), calls=%async_computation.1 | async-start | bytes 1572864 | tf_op jit(solution)/shard_map/all_gather | solution.py:61
  69.7 8.4 %copy-start.8 = (f32[8,2,4,2048]{3,2,1,0:T(4,128)S(1)}, f32[8,2,4,2048]{3,2,1,0:T(4,128)}, u32[]{:S(2)}) copy-start(f32[8,2,4,2048]{3,2,1,0:T(4,128)} %reshape_reshape.38) | copy-start | bytes 1572868
  69.7 9.9 %copy-start.12 = (f32[1,1,32,2048]{3,2,1,0:T(8,128)S(1)}, f32[1,1,32,2048]{3,2,1,0:T(8,128)}, u32[]{:S(2)}) copy-start(f32[1,1,32,2048]{3,2,1,0:T(8,128)} %slice_multiply_fusion.13) | copy-start | bytes 786436
  71.5 17.7 %collective-permute-start.5 = (f32[64,2048]{1,0:T(8,128)}, f32[64,2048]{1,0:T(8,128)}, u32[]{:S(2)}, u32[]{:S(2)}) collective-permute-start(f32[64,2048]{1,0:T(8,128)} %get-tuple-element.19), channel_id=1, source_target_pairs={{0,64},{2,66},{4,68},{6,70},{8,72},{10,74},{12,76},{14,78},{16,80}... | collective-permute-start | bytes 1572872 | tf_op jit(solution)/shard_map/ppermute | solution.py:12
  74.7 23.9 %collective-permute-start.4 = (f32[64,2048]{1,0:T(8,128)}, f32[64,2048]{1,0:T(8,128)}, u32[]{:S(2)}, u32[]{:S(2)}) collective-permute-start(f32[64,2048]{1,0:T(8,128)} %get-tuple-element.15), channel_id=1, source_target_pairs={{0,32},{2,34},{4,36},{6,38},{8,40},{10,42},{12,44},{14,46},{16,48}... | collective-permute-start | bytes 1572872 | tf_op jit(solution)/shard_map/ppermute | solution.py:12
  75.4 23.2 %collective-permute-start.3 = (f32[64,2048]{1,0:T(8,128)}, f32[64,2048]{1,0:T(8,128)}, u32[]{:S(2)}, u32[]{:S(2)}) collective-permute-start(f32[64,2048]{1,0:T(8,128)} %get-tuple-element.16), channel_id=1, source_target_pairs={{0,16},{2,18},{4,20},{6,22},{8,24},{10,26},{12,28},{14,30},{16,0},... | collective-permute-start | bytes 1572872 | tf_op jit(solution)/shard_map/ppermute | solution.py:12
  75.4 24.8 %collective-permute-start.2 = (f32[64,2048]{1,0:T(8,128)}, f32[64,2048]{1,0:T(8,128)}, u32[]{:S(2)}, u32[]{:S(2)}) collective-permute-start(f32[64,2048]{1,0:T(8,128)} %get-tuple-element.17), channel_id=1, source_target_pairs={{0,8},{2,10},{4,12},{6,14},{8,0},{10,2},{12,4},{14,6},{16,24},{18,... | collective-permute-start | bytes 1572872 | tf_op jit(solution)/shard_map/ppermute | solution.py:12
  77.6 22.6 %collective-permute-start.1 = (f32[64,2048]{1,0:T(8,128)}, f32[64,2048]{1,0:T(8,128)}, u32[]{:S(2)}, u32[]{:S(2)}) collective-permute-start(f32[64,2048]{1,0:T(8,128)} %get-tuple-element.18), channel_id=1, source_target_pairs={{0,4},{2,6},{4,0},{6,2},{8,12},{10,14},{12,8},{14,10},{16,20},{18,... | collective-permute-start | bytes 1572872 | tf_op jit(solution)/shard_map/ppermute | solution.py:12
  89.3 11.0 %collective-permute-start = (f32[64,2048]{1,0:T(8,128)}, f32[64,2048]{1,0:T(8,128)}, u32[]{:S(2)}, u32[]{:S(2)}) collective-permute-start(f32[64,2048]{1,0:T(8,128)} %get-tuple-element.14), channel_id=1, source_target_pairs={{0,2},{2,0},{4,6},{6,4},{8,10},{10,8},{12,14},{14,12},{16,18},{18,... | collective-permute-start | bytes 1572872 | tf_op jit(solution)/shard_map/ppermute | solution.py:12
  143.6 8.5 %copy-start.10 = (f32[2,2,16,2048]{3,2,1,0:T(8,128)S(1)}, f32[2,2,16,2048]{3,2,1,0:T(8,128)}, u32[]{:S(2)}) copy-start(f32[2,2,16,2048]{3,2,1,0:T(8,128)} %reshape_reshape.46) | copy-start | bytes 1572868
  143.7 9.8 %copy-start.9 = (f32[4,2,8,2048]{3,2,1,0:T(8,128)S(1)}, f32[4,2,8,2048]{3,2,1,0:T(8,128)}, u32[]{:S(2)}) copy-start(f32[4,2,8,2048]{3,2,1,0:T(8,128)} %reshape_reshape.45) | copy-start | bytes 1572868
  154.9 9.0 %copy-start.7 = (f32[8,2,4,2048]{3,2,1,0:T(4,128)S(1)}, f32[8,2,4,2048]{3,2,1,0:T(4,128)}, u32[]{:S(2)}) copy-start(f32[8,2,4,2048]{3,2,1,0:T(4,128)} %reshape_reshape.44) | copy-start | bytes 1572868
  154.9 9.7 %copy-start.6 = (f32[32,2,1,2048]{3,1,0,2:T(2,128)S(1)}, f32[32,2,1,2048]{3,1,0,2:T(2,128)}, u32[]{:S(2)}) copy-start(f32[32,2,1,2048]{3,1,0,2:T(2,128)} %reshape_reshape.42) | copy-start | bytes 1572868
  154.9 10.5 %copy-start.14 = (f32[1,1,32,2048]{3,2,1,0:T(8,128)S(1)}, f32[1,1,32,2048]{3,2,1,0:T(8,128)}, u32[]{:S(2)}) copy-start(f32[1,1,32,2048]{3,2,1,0:T(8,128)} %slice_multiply_fusion.1) | copy-start | bytes 786436
  156.9 8.6 %copy-start.15 = (f32[8,1,4,2048]{3,2,1,0:T(4,128)S(1)}, f32[8,1,4,2048]{3,2,1,0:T(4,128)}, u32[]{:S(2)}) copy-start(f32[8,1,4,2048]{3,2,1,0:T(4,128)} %slice_multiply_fusion.7) | copy-start | bytes 786436
  156.9 16.6 %collective-permute-start.11 = (f32[64,2048]{1,0:T(8,128)}, f32[64,2048]{1,0:T(8,128)}, u32[]{:S(2)}, u32[]{:S(2)}) collective-permute-start(f32[64,2048]{1,0:T(8,128)} %get-tuple-element.9), channel_id=1, source_target_pairs={{0,64},{2,66},{4,68},{6,70},{8,72},{10,74},{12,76},{14,78},{16,80}... | collective-permute-start | bytes 1572872 | tf_op jit(solution)/shard_map/ppermute | solution.py:12
  159.9 23.8 %collective-permute-start.10 = (f32[64,2048]{1,0:T(8,128)}, f32[64,2048]{1,0:T(8,128)}, u32[]{:S(2)}, u32[]{:S(2)}) collective-permute-start(f32[64,2048]{1,0:T(8,128)} %get-tuple-element.10), channel_id=1, source_target_pairs={{0,32},{2,34},{4,36},{6,38},{8,40},{10,42},{12,44},{14,46},{16,48}... | collective-permute-start | bytes 1572872 | tf_op jit(solution)/shard_map/ppermute | solution.py:12
  160.5 23.2 %collective-permute-start.9 = (f32[64,2048]{1,0:T(8,128)}, f32[64,2048]{1,0:T(8,128)}, u32[]{:S(2)}, u32[]{:S(2)}) collective-permute-start(f32[64,2048]{1,0:T(8,128)} %get-tuple-element.11), channel_id=1, source_target_pairs={{0,16},{2,18},{4,20},{6,22},{8,24},{10,26},{12,28},{14,30},{16,0},... | collective-permute-start | bytes 1572872 | tf_op jit(solution)/shard_map/ppermute | solution.py:12
  160.9 24.7 %collective-permute-start.8 = (f32[64,2048]{1,0:T(8,128)}, f32[64,2048]{1,0:T(8,128)}, u32[]{:S(2)}, u32[]{:S(2)}) collective-permute-start(f32[64,2048]{1,0:T(8,128)} %get-tuple-element.12), channel_id=1, source_target_pairs={{0,8},{2,10},{4,12},{6,14},{8,0},{10,2},{12,4},{14,6},{16,24},{18,... | collective-permute-start | bytes 1572872 | tf_op jit(solution)/shard_map/ppermute | solution.py:12
  163.1 22.6 %collective-permute-start.7 = (f32[64,2048]{1,0:T(8,128)}, f32[64,2048]{1,0:T(8,128)}, u32[]{:S(2)}, u32[]{:S(2)}) collective-permute-start(f32[64,2048]{1,0:T(8,128)} %get-tuple-element.13), channel_id=1, source_target_pairs={{0,4},{2,6},{4,0},{6,2},{8,12},{10,14},{12,8},{14,10},{16,20},{18,... | collective-permute-start | bytes 1572872 | tf_op jit(solution)/shard_map/ppermute | solution.py:12
  166.2 9.5 %copy-start.5 = (f32[8,8,8,256]{3,2,1,0:T(8,128)S(1)}, f32[8,8,8,256]{3,2,1,0:T(8,128)}, u32[]{:S(2)}) copy-start(f32[8,8,8,256]{3,2,1,0:T(8,128)} %fusion.15) | copy-start | bytes 1572868
  173.6 12.1 %collective-permute-start.6 = (f32[64,2048]{1,0:T(8,128)}, f32[64,2048]{1,0:T(8,128)}, u32[]{:S(2)}, u32[]{:S(2)}) collective-permute-start(f32[64,2048]{1,0:T(8,128)} %get-tuple-element.8), channel_id=1, source_target_pairs={{0,2},{2,0},{4,6},{6,4},{8,10},{10,8},{12,14},{14,12},{16,18},{18,... | collective-permute-start | bytes 1572872 | tf_op jit(solution)/shard_map/ppermute | solution.py:12
  (9 other events, 41.0 us)
Sparse Core Ops, SparseCore 0:
  9.0 25.1 all-gather.2
  103.8 23.6 all-gather.4
where the time goes:
time: 200 us; the launch traced here: 196 us
  other arithmetic  62.4 us (31%)
  local copies, waits for them, and re-layouts  31.7 us (16%)
  waiting for transfers between devices  30.1 us (15%)
  between operations  29.6 us (15%)
  matrix products  28.5 us (14%)
  starting transfers between devices  13.7 us (7%)
    dot_general x4, matrix products, apply_blocks(): jnp.einsum('pcjt,cjts->pcs', chosen, blocks, precision=lax.Precision.HIGH...  28.5 us
    mul x12, other arithmetic, bit_terms(): fail[first + bit] * lower[:, 0]  16 us
    mul x12, other arithmetic, bit_terms(): repair[first + bit] * upper[:, 1]  15.3 us
    ppermute x12, waiting for transfers between devices, from_partner(): return lax.ppermute(value, axis, pairs)  15.1 us
    all_gather x2, waiting for transfers between devices, local(): whole = lax.all_gather(current, 'queue', axis=1, tiled=True)  14.2 us
    ppermute x12, starting transfers between devices, from_partner(): return lax.ppermute(value, axis, pairs)  13.6 us
    another operation x12, local copies, waits for them, and re-layouts, bit_terms(): lower = killed.reshape(shape)  11 us
    another operation x12, other arithmetic, bit_terms(): jnp.stack((repair[first + bit] * upper[:, 1], fail[first + bit] * lower[:...  9.75 us
  transfers between devices with their start and end apart: 14, of which 6 were waited for; matrix products, arithmetic and copies ran while one was open for 31% of the time, Pallas kernels for 0%

commit v1 on v0

v1 whole, which is shorter than its diff:
```python
import functools

import jax
import jax.numpy as jnp
from jax import lax
from jax.experimental import pallas as pl
from jax.experimental.pallas import tpu as pltpu
from jax.sharding import PartitionSpec as P

STEPS = 2
RACKS = 12
LOW = 6
CH = 2
R = 32
NB = 8
BS = 256
PIECES = 4
PB = NB // PIECES
SLOTS = 4
KINDS = 8
AG, YA, ZA, YB, ZB, CO, XF, XH = range(KINDS)
MESH = pl.DeviceIdType.MESH
F32 = jnp.float32
BF16 = jnp.bfloat16


def kernel(
    st, qw, kw, qrows, krows, rindex, rtable, out,
    vw, vhl, kb, qb, rya, rza, sy, sz, ryb, rzb, rco, rxf, rxh, ob,
    wst, whi, wlo, coef, rowc, diag,
    ssem, rsem, wsem, lsem, osem,
):
    rack = lax.axis_index("rack")
    me_q = lax.axis_index("queue")
    co = rack % 2
    xh = (rack // 2) % 2
    z0 = (rack // 4) % 2
    z1 = (rack // 8) % 2
    y0 = (rack // 16) % 2
    y1 = (rack // 32) % 2
    oq = 1 - me_q
    d_x1 = (rack, oq)
    d_x3 = (rack + 2 - 4 * xh, oq)
    d_co = (rack + 1 - 2 * co, me_q)
    d_z1 = (rack + 4 - 8 * z0, me_q)
    d_z3 = (rack + 4 - 8 * z0 + 8 - 16 * z1, me_q)
    d_y1 = (rack + 16 - 32 * y0, me_q)
    d_y3 = (rack + 16 - 32 * y0 + 32 - 64 * y1, me_q)
    own = me_q * NB
    other = oq * NB

    def load(ch, b):
        return pltpu.make_async_copy(
            st.at[pl.ds(ch * R, R), pl.ds(b * BS, BS)], vw.at[0, ch, own + b], lsem.at[ch, b]
        )

    for ch in range(CH):
        for b in range(NB):
            load(ch, b).start()

    def weight(u):
        src = qw if u % 2 == 0 else kw
        return pltpu.make_async_copy(src.at[u // 2], wst.at[u % SLOTS], wsem.at[u % SLOTS])

    for u in range(SLOTS):
        weight(u).start()

    barrier = pltpu.get_barrier_semaphore()
    partners = (d_x1, d_x3, d_co, d_z1, d_z3, d_y1, d_y3)
    for d in partners:
        pl.semaphore_signal(barrier, inc=1, device_id=d, device_id_type=MESH)

    fail = [rtable[0, rindex[r]] for r in range(RACKS)]
    repair = [rtable[1, rindex[r]] for r in range(RACKS)]
    total = 1.0
    for r in range(RACKS):
        total = total + (fail[r] + repair[r])
    inv = 1.0 / jnp.full((8, BS), total, F32)
    for r in range(RACKS):
        coef[r] = fail[r] * inv
        coef[RACKS + r] = repair[r] * inv
    coef[24] = inv
    pick = lambda flag, a, b: jnp.where(flag == 1, a, b)
    coef[25] = pick(co, fail[6], repair[6]) * inv
    coef[26] = pick(xh, fail[7], repair[7]) * inv
    coef[27] = pick(y0, 0.0, fail[10]) * inv
    coef[28] = pick(y0, repair[10], 0.0) * inv
    coef[29] = pick(y1, fail[11], repair[11]) * inv
    coef[30] = pick(z0, 0.0, fail[8]) * inv
    coef[31] = pick(z0, repair[8], 0.0) * inv
    coef[32] = pick(z1, fail[9], repair[9]) * inv
    sub = lax.broadcasted_iota(jnp.int32, (8, BS), 0)
    for b in range(3):
        bit = (sub // 2**b) % 2
        rowc[b] = jnp.where(bit == 1, fail[b] * inv, 0.0)
        rowc[3 + b] = jnp.where(bit == 0, repair[b] * inv, 0.0)
    high = (
        pick(co, repair[6], fail[6]) + pick(xh, repair[7], fail[7])
        + pick(z0, repair[8], fail[8]) + pick(z1, repair[9], fail[9])
        + pick(y0, repair[10], fail[10]) + pick(y1, repair[11], fail[11])
    )
    for ch in range(CH):
        for i in range(R // 8):
            ex = high + (repair[5] if ch else fail[5])
            ex = ex + (repair[3] if i % 2 else fail[3]) + (repair[4] if i // 2 else fail[4])
            leave = jnp.full((8, BS), ex, F32)
            for b in range(3):
                leave = leave + jnp.where((sub // 2**b) % 2 == 1, repair[b], fail[b])
            diag[ch, i] = 1.0 - leave * inv

    def rdma(kind, s, ch, p, src, dst, dev):
        return pltpu.make_async_remote_copy(
            src_ref=src, dst_ref=dst, send_sem=ssem.at[kind, s, ch, p],
            recv_sem=rsem.at[kind, s, ch, p], device_id=dev, device_id_type=MESH,
        )

    def blocks(ref, s, ch, p):
        return ref.at[s, ch, pl.ds(p * PB, PB)]

    def mine(s, ch, p):
        return vw.at[s, ch, pl.ds(own + p * PB, PB)]

    def copy(kind, s, ch, p, src=None):
        if src is None:
            src = blocks(kb, s, ch, p)
        if kind == AG:
            return rdma(kind, s, ch, p, mine(s, ch, p), mine(s, ch, p), d_x1)
        dst, dev = {
            YA: (rya, d_y3), ZA: (rza, d_z3), YB: (ryb, d_y1), ZB: (rzb, d_z1), CO: (rco, d_co),
        }[kind]
        return rdma(kind, s, ch, p, src, blocks(dst, s, ch, p), dev)

    def relay(s, ch, p, src):
        return rdma(XF, s, ch, p, src, rxf.at[s, ch, pl.ds((p * PB) % (NB // 2), PB)],
                    d_x1 if p < PIECES // 2 else d_x3)

    def relayed(s, ch, p):
        return rxf.at[s, ch, pl.ds((p * PB) % (NB // 2), PB)]

    def final_x(s, ch, p, src, dev, sent=XH):
        return pltpu.make_async_remote_copy(
            src_ref=src, dst_ref=blocks(rxh, s, ch, p), send_sem=ssem.at[sent, s, ch, p],
            recv_sem=rsem.at[XH, s, ch, p], device_id=dev, device_id_type=MESH,
        )

    def send_c(s, ch, p):
        copy(AG, s, ch, p).start()

        @pl.when(y1 == 1)
        def _():
            copy(YA, s, ch, p, mine(s, ch, p)).start()

        @pl.when(z1 == 1)
        def _():
            copy(ZA, s, ch, p, mine(s, ch, p)).start()

        @pl.when(co == 1)
        def _():
            copy(CO, s, ch, p, mine(s, ch, p)).start()

    def send_k(s, ch, p):
        @pl.when(xh == 0)
        def _():
            relay(s, ch, p, blocks(kb, s, ch, p)).start()

        @pl.when(y1 == 0)
        def _():
            copy(YA, s, ch, p).start()

        @pl.when(z1 == 0)
        def _():
            copy(ZA, s, ch, p).start()

        @pl.when(co == 0)
        def _():
            copy(CO, s, ch, p).start()

    def split_block(s, ch, b):
        x = vw[s, ch, b]
        hi = x.astype(BF16)
        vhl[b, :R, :] = hi
        vhl[b, R:, :] = (x - hi.astype(F32)).astype(BF16)

    def recv_ag(s, ch):
        @pl.loop(0, NB)
        def _(b):
            split_block(s, ch, own + b)

        for p in range(PIECES):
            theirs = vw.at[s, ch, pl.ds(other + p * PB, PB)]
            rdma(AG, s, ch, p, theirs, theirs, d_x1).wait_recv()

            @pl.when(xh == 1)
            def _(p=p, theirs=theirs):
                final_x(s, ch, p, theirs, d_x3).start()

            @pl.loop(0, PB)
            def _(b, p=p):
                split_block(s, ch, other + p * PB + b)

    def product(rows, c, m):
        lhs = jnp.concatenate([vhl[rows[c, j]] for j in range(3)], axis=1)
        a = jnp.dot(lhs, whi[m, c], preferred_element_type=F32)
        b = jnp.dot(lhs[:R], wlo[m, c], preferred_element_type=F32)
        return a[:R] + a[R:] + b

    def mm(s, ch, p):
        @pl.loop(p * PB, (p + 1) * PB)
        def _(c):
            kb[s, ch, c] = product(krows, c, 1)
            qb[ch, c] = product(qrows, c, 0)

        send_k(s, ch, p)

    def forward(s, ch, p):
        if p < PIECES // 2:
            @pl.when(xh == 0)
            def _():
                relay(s, ch, p, relayed(s, ch, p)).wait_recv()
                final_x(s, ch, p, relayed(s, ch, p), d_x3).start()
        else:
            @pl.when(xh == 1)
            def _():
                relay(s, ch, p, relayed(s, ch, p)).wait_recv()
                final_x(s, ch, p, relayed(s, ch, p), d_x1, XF).start()

    def sums(s, ch, p):
        forward(s, ch, p)
        for kind, recv, send, at, nxt in ((YA, rya, sy, 27, YB), (ZA, rza, sz, 30, ZB)):
            copy(kind, s, ch, p).wait_recv()

            @pl.loop(0, PB)
            def _(b, recv=recv, send=send, at=at):
                c = p * PB + b
                ca, cb, cc = coef[at], coef[at + 1], coef[at + 2]
                for i in range(R // 8):
                    rs = pl.ds(i * 8, 8)
                    send[s, ch, c, rs, :] = (
                        ca * kb[s, ch, c, rs, :] + cb * vw[s, ch, own + c, rs, :] + cc * recv[s, ch, c, rs, :]
                    )

            copy(nxt, s, ch, p, blocks(send, s, ch, p)).start()

    def comb(s, ch, p):
        for kind in (CO, YB, ZB):
            copy(kind, s, ch, p).wait_recv()
        final_x(s, ch, p, blocks(rxh, s, ch, p), d_x3).wait_recv()

        @pl.loop(0, PB)
        def _(b):
            c = p * PB + b
            n = R // 8
            rs = [pl.ds(i * 8, 8) for i in range(n)]
            cur = [vw[s, ch, own + c, r, :] for r in rs]
            kil = [kb[s, ch, c, r, :] for r in rs]
            for i in range(n):
                acc = diag[ch, i] * cur[i] + coef[24] * qb[ch, c, rs[i], :]
                for t in range(3):
                    acc = acc + rowc[t] * pltpu.roll(kil[i], 2**t, 0)
                    acc = acc + rowc[3 + t] * pltpu.roll(cur[i], 8 - 2**t, 0)
                acc = acc + (coef[3] * kil[i - 1] if i % 2 else coef[15] * cur[i + 1])
                acc = acc + (coef[4] * kil[i - 2] if i // 2 else coef[16] * cur[i + 2])
                if ch == 0:
                    acc = acc + coef[17] * vw[s, 1, own + c, rs[i], :]
                else:
                    acc = acc + coef[5] * kb[s, 0, c, rs[i], :]
                acc = acc + coef[25] * rco[s, ch, c, rs[i], :]
                acc = acc + coef[26] * rxh[s, ch, c, rs[i], :]
                acc = acc + ryb[s, ch, c, rs[i], :] + rzb[s, ch, c, rs[i], :]
                if s + 1 < STEPS:
                    vw[s + 1, ch, own + c, rs[i], :] = acc
                else:
                    ob[ch, c, rs[i], :] = acc

        if s + 1 < STEPS:
            send_c(s + 1, ch, p)
        else:
            for b in range(PB):
                store(ch, p * PB + b).start()

    def store(ch, b):
        return pltpu.make_async_copy(
            ob.at[ch, b], out.at[pl.ds(ch * R, R), pl.ds(b * BS, BS)], osem.at[ch, b]
        )

    for b in range(NB):
        load(0, b).wait()
    pl.semaphore_wait(barrier, len(partners))
    for p in range(PIECES):
        send_c(0, 0, p)
    for b in range(NB):
        load(1, b).wait()
    for p in range(PIECES):
        send_c(0, 1, p)

    for u in range(2 * NB):
        weight(u).wait()

        @pl.loop(0, 24)
        def _(i, u=u):
            rs = pl.ds(pl.multiple_of(i * 32, 32), 32)
            x = wst[u % SLOTS, rs, :]
            hi = x.astype(BF16)
            whi[u % 2, u // 2, rs, :] = hi
            wlo[u % 2, u // 2, rs, :] = (x - hi.astype(F32)).astype(BF16)

        if u + SLOTS < 2 * NB:
            weight(u + SLOTS).start()

    every = range(PIECES)

    def products(s, ch):
        recv_ag(s, ch)
        for p in every:
            mm(s, ch, p)

    def all_of(f, s, ch):
        for p in every:
            f(s, ch, p)

    products(0, 0)
    all_of(sums, 0, 0)
    products(0, 1)
    all_of(comb, 0, 0)
    all_of(sums, 0, 1)
    all_of(comb, 0, 1)
    products(1, 0)
    all_of(sums, 1, 0)
    products(1, 1)
    all_of(comb, 1, 0)
    all_of(sums, 1, 1)
    all_of(comb, 1, 1)

    for s in range(STEPS):
        for ch in range(CH):
            for p in every:
                for kind in (AG, YA, ZA, YB, ZB, CO):
                    copy(kind, s, ch, p).wait_send()

                first = p < PIECES // 2
                for kind, sender in ((XF, 0 if first else None), (XH, 1 if not first else None)):
                    if sender is None:
                        final_x(s, ch, p, relayed(s, ch, p), d_x3, kind).wait_send()
                    else:
                        @pl.when(xh == sender)
                        def _(s=s, ch=ch, p=p, kind=kind):
                            final_x(s, ch, p, relayed(s, ch, p), d_x3, kind).wait_send()

    for ch in range(CH):
        for b in range(NB):
            store(ch, b).wait()


def local(state, queue_blocks, queue_rows, kill_blocks, kill_rows, rate_index, rate_table):
    buf = lambda *shape: pltpu.VMEM(shape, F32)
    full = (STEPS, CH, NB, R, BS)
    return pl.pallas_call(
        kernel,
        out_shape=jax.ShapeDtypeStruct(state.shape, F32),
        in_specs=[pl.BlockSpec(memory_space=pl.ANY)] * 3
        + [pl.BlockSpec(memory_space=pltpu.SMEM)] * 4,
        out_specs=pl.BlockSpec(memory_space=pl.ANY),
        scratch_shapes=[
            buf(STEPS, CH, 2 * NB, R, BS),
            pltpu.VMEM((2 * NB, 2 * R, BS), BF16),
            buf(*full),
            buf(CH, NB, R, BS),
            buf(*full), buf(*full),
            buf(*full), buf(*full),
            buf(*full), buf(*full),
            buf(*full),
            buf(STEPS, CH, NB // 2, R, BS),
            buf(*full),
            buf(CH, NB, R, BS),
            buf(SLOTS, 3 * BS, BS),
            pltpu.VMEM((2, NB, 3 * BS, BS), BF16),
            pltpu.VMEM((2, NB, 3 * BS, BS), BF16),
            buf(33, 8, BS), buf(6, 8, BS), buf(CH, R // 8, 8, BS),
            pltpu.SemaphoreType.DMA((KINDS, STEPS, CH, PIECES)),
            pltpu.SemaphoreType.DMA((KINDS, STEPS, CH, PIECES)),
            pltpu.SemaphoreType.DMA((SLOTS,)),
            pltpu.SemaphoreType.DMA((CH, NB)),
            pltpu.SemaphoreType.DMA((CH, NB)),
        ],
        compiler_params=pltpu.CompilerParams(
            collective_id=0, has_side_effects=True, vmem_limit_bytes=60 * 1024 * 1024
        ),
        name="chain",
    )(
        state,
        queue_blocks.reshape(NB, 3 * BS, BS),
        kill_blocks.reshape(NB, 3 * BS, BS),
        queue_rows, kill_rows, rate_index, rate_table.T,
    )


def solution(mesh):
    placed = (
        P("rack", "queue"),
        P("queue", None, None, None),
        P("queue", None),
        P("queue", None, None, None),
        P("queue", None),
        P(),
        P(),
    )
    return jax.shard_map(
        local, mesh=mesh, in_specs=placed, out_specs=P("rack", "queue"), check_vma=False
    )
```

time: 200 us -> 59.5 us (0.30); the launches traced: 196 us -> 58.6 us
  other arithmetic: 62.4 us -> 0 us
  Pallas kernels: 0 us -> 54.1 us
  waiting for transfers between devices: 30.1 us -> 0 us
  between operations: 29.6 us -> 0.01 us
  matrix products: 28.5 us -> 0 us
  local copies, waits for them, and re-layouts: 31.7 us -> 4.57 us
  starting transfers between devices: 13.7 us -> 0 us
    pallas_call x0 -> x1, Pallas kernels: none -> 54.1 us  [local(): pl.pallas_call(kernel, out_shape=jax.ShapeDtypeStruct(state.shape, F32),...]
    mul x24 -> x0, other arithmetic: 31.3 us -> none  [the longest x12 16 us: bit_terms(): fail[first + bit] * lower[:, 0]]
    dot_general x4 -> x0, matrix products: 28.5 us -> none  [apply_blocks(): jnp.einsum('pcjt,cjts->pcs', chosen, blocks, precision=lax.Precision.HIGH...]
    ppermute x12 -> x0, waiting for transfers between devices: 15.1 us -> none  [from_partner(): return lax.ppermute(value, axis, pairs)]
    all_gather x2 -> x0, waiting for transfers between devices: 14.2 us -> none  [local(): whole = lax.all_gather(current, 'queue', axis=1, tiled=True)]
    add x3 -> x0, other arithmetic: 14.2 us -> none  [the longest x1 7.42 us: local(): leaving + jnp.where(flag == 1, repair[low_count + bit], fail[low_count +...]
    ppermute x12 -> x0, starting transfers between devices: 13.6 us -> none  [from_partner(): return lax.ppermute(value, axis, pairs)]
    another operation x12 -> x0, local copies, waits for them, and re-layouts: 11 us -> none  [bit_terms(): lower = killed.reshape(shape)]
  transfers between devices with their start and end apart: 14 -> 0, of which waited for: 6 -> 0; matrix products, arithmetic and copies ran while one was open for 31% -> 0% of each run, Pallas kernels for 0% -> 0%
where the time goes in v1:
time: 59.5 us; the launch traced here: 58.6 us
  Pallas kernels  54.1 us (91%)
  local copies, waits for them, and re-layouts  4.57 us (8%)
    pallas_call x1, Pallas kernels, local(): pl.pallas_call(kernel, out_shape=jax.ShapeDtypeStruct(state.shape, F32),...  54.1 us
    unnamed x3, local copies, waits for them, and re-layouts  4.57 us

profile of v1, /device:TPU:68, one launch (start us, length us, event | category | flops | bytes accessed | tf_op | source)
XLA Modules:
  0.0 58.6 jit_solution(10857893467861233100)
XLA Ops:
  0.0 1.3 %copy.8.qrows = s32[8,3]{1,0:T(8,128)} copy(s32[8,3]{0,1:T(4,128)} %param.9) | data formatting | bytes 192 | tf_op args[2]
  1.3 1.3 %copy.9.krows = s32[8,3]{1,0:T(8,128)} copy(s32[8,3]{0,1:T(4,128)} %param.11) | data formatting | bytes 192 | tf_op args[4]
  2.7 54.1 %chain.1 = f32[64,2048]{1,0:T(8,128)} custom-call(f32[64,2048]{1,0:T(8,128)} %st.1, f32[8,768,256]{2,1,0:T(8,128)} %bitcast.3, f32[8,768,256]{2,1,0:T(8,128)} %bitcast.4, s32[8,3]{1,0:T(8,128)} %copy.8.qrows, s32[8,3]{1,0:T(8,128)} %copy.9.krows, s32[12]{0:T(128)} %rindex.1, f32[2,8]{1,0:T(2,128)} %bitcast.5), custom_call_target="tpu_custom_call" | custom-call | tf_op jit(solution)/shard_map/chain/pallas_call | solution.py:357
  56.8 1.9 %copy.11 = f32[64,2048]{1,0:T(8,128)} copy(f32[64,2048]{1,0:T(8,128)} %chain.1) | data formatting | bytes 1048576

commit v2 on v1

--- a/solution.py
+++ b/solution.py
@@ -16,7 +16,7 @@
 BS = 256
 PIECES = 4
 PB = NB // PIECES
-SLOTS = 4
+SLOTS = 2 * NB
 KINDS = 8
 AG, YA, ZA, YB, ZB, CO, XF, XH = range(KINDS)
 MESH = pl.DeviceIdType.MESH
@@ -59,8 +59,8 @@
             load(ch, b).start()
 
     def weight(u):
-        src = qw if u % 2 == 0 else kw
-        return pltpu.make_async_copy(src.at[u // 2], wst.at[u % SLOTS], wsem.at[u % SLOTS])
+        src = kw if u < NB else qw
+        return pltpu.make_async_copy(src.at[u % NB], wst.at[u], wsem.at[u])
 
     for u in range(SLOTS):
         weight(u).start()
@@ -199,18 +199,22 @@
                 split_block(s, ch, other + p * PB + b)
 
     def product(rows, c, m):
-        lhs = jnp.concatenate([vhl[rows[c, j]] for j in range(3)], axis=1)
+        lhs = jnp.concatenate([vhl[rows[j, c]] for j in range(3)], axis=1)
         a = jnp.dot(lhs, whi[m, c], preferred_element_type=F32)
         b = jnp.dot(lhs[:R], wlo[m, c], preferred_element_type=F32)
         return a[:R] + a[R:] + b
 
-    def mm(s, ch, p):
+    def kill(s, ch, p):
         @pl.loop(p * PB, (p + 1) * PB)
         def _(c):
             kb[s, ch, c] = product(krows, c, 1)
+
+        send_k(s, ch, p)
+
+    def queue(ch):
+        @pl.loop(0, NB)
+        def _(c):
             qb[ch, c] = product(qrows, c, 0)
-
-        send_k(s, ch, p)
 
     def forward(s, ch, p):
         if p < PIECES // 2:
@@ -225,7 +229,6 @@
                 final_x(s, ch, p, relayed(s, ch, p), d_x1, XF).start()
 
     def sums(s, ch, p):
-        forward(s, ch, p)
         for kind, recv, send, at, nxt in ((YA, rya, sy, 27, YB), (ZA, rza, sz, 30, ZB)):
             copy(kind, s, ch, p).wait_recv()
 
@@ -293,43 +296,46 @@
     for p in range(PIECES):
         send_c(0, 1, p)
 
-    for u in range(2 * NB):
-        weight(u).wait()
-
-        @pl.loop(0, 24)
-        def _(i, u=u):
-            rs = pl.ds(pl.multiple_of(i * 32, 32), 32)
-            x = wst[u % SLOTS, rs, :]
-            hi = x.astype(BF16)
-            whi[u % 2, u // 2, rs, :] = hi
-            wlo[u % 2, u // 2, rs, :] = (x - hi.astype(F32)).astype(BF16)
-
-        if u + SLOTS < 2 * NB:
-            weight(u + SLOTS).start()
+    def weights(m):
+        for c in range(NB):
+            u = (1 - m) * NB + c
+            weight(u).wait()
+
+            @pl.loop(0, 24)
+            def _(i, u=u, c=c):
+                rs = pl.ds(pl.multiple_of(i * 32, 32), 32)
+                x = wst[u, rs, :]
+                hi = x.astype(BF16)
+                whi[m, c, rs, :] = hi
+                wlo[m, c, rs, :] = (x - hi.astype(F32)).astype(BF16)
 
     every = range(PIECES)
-
-    def products(s, ch):
-        recv_ag(s, ch)
+    early, late = every[: PIECES // 2], every[PIECES // 2 :]
+
+    def all_of(f, s, ch, pieces=every):
+        for p in pieces:
+            f(s, ch, p)
+
+    weights(1)
+    for s in range(STEPS):
+        recv_ag(s, 0)
+        all_of(kill, s, 0)
+        if s == 0:
+            weights(0)
+        queue(0)
+        all_of(sums, s, 0, early)
+        all_of(forward, s, 0, late)
+        recv_ag(s, 1)
+        all_of(kill, s, 1)
+        all_of(sums, s, 0, late)
+        all_of(forward, s, 0, early)
+        queue(1)
         for p in every:
-            mm(s, ch, p)
-
-    def all_of(f, s, ch):
-        for p in every:
-            f(s, ch, p)
-
-    products(0, 0)
-    all_of(sums, 0, 0)
-    products(0, 1)
-    all_of(comb, 0, 0)
-    all_of(sums, 0, 1)
-    all_of(comb, 0, 1)
-    products(1, 0)
-    all_of(sums, 1, 0)
-    products(1, 1)
-    all_of(comb, 1, 0)
-    all_of(sums, 1, 1)
-    all_of(comb, 1, 1)
+            comb(s, 0, p)
+            sums(s, 1, p)
+        all_of(forward, s, 1, late)
+        all_of(forward, s, 1, early)
+        all_of(comb, s, 1)
 
     for s in range(STEPS):
         for ch in range(CH):
@@ -390,7 +396,7 @@
         state,
         queue_blocks.reshape(NB, 3 * BS, BS),
         kill_blocks.reshape(NB, 3 * BS, BS),
-        queue_rows, kill_rows, rate_index, rate_table.T,
+        queue_rows.T, kill_rows.T, rate_index, rate_table.T,
     )
 
 

time: 59.5 us -> 57.5 us (0.966)
  local copies, waits for them, and re-layouts: 4.57 us -> 1.87 us
  Pallas kernels: 54.1 us -> 54.8 us
    unnamed x3 -> x1, local copies, waits for them, and re-layouts: 4.57 us -> 1.87 us
    pallas_call x1, Pallas kernels: 54.1 us -> 54.8 us  [local(): pl.pallas_call(kernel, out_shape=jax.ShapeDtypeStruct(state.shape, F32),...]
where the time goes in v2:
time: 57.5 us; the launch traced here: 56.7 us
  Pallas kernels  54.8 us (95%)
  local copies, waits for them, and re-layouts  1.87 us (3%)
    pallas_call x1, Pallas kernels, local(): pl.pallas_call(kernel, out_shape=jax.ShapeDtypeStruct(state.shape, F32),...  54.8 us
    unnamed x1, local copies, waits for them, and re-layouts  1.87 us

profile of v2, /device:TPU:68, one launch (start us, length us, event | category | flops | bytes accessed | tf_op | source)
XLA Modules:
  0.0 56.7 jit_solution(8464648704825269925)
XLA Ops:
  0.0 54.8 %chain.1 = f32[64,2048]{1,0:T(8,128)} custom-call(f32[64,2048]{1,0:T(8,128)} %st.1, f32[8,768,256]{2,1,0:T(8,128)} %bitcast.5, f32[8,768,256]{2,1,0:T(8,128)} %bitcast.6, s32[3,8]{1,0:T(4,128)} %bitcast.7, s32[3,8]{1,0:T(4,128)} %bitcast.8, s32[12]{0:T(128)} %rindex.1, f32[2,8]{1,0:T(2,128)} %bitcast.9), custom_call_target="tpu_custom_call" | custom-call | tf_op jit(solution)/shard_map/chain/pallas_call | solution.py:363
  54.8 1.9 %copy.9 = f32[64,2048]{1,0:T(8,128)} copy(f32[64,2048]{1,0:T(8,128)} %chain.1) | data formatting | bytes 1048576

commit v3 on v2

--- a/solution.py
+++ b/solution.py
@@ -178,8 +178,8 @@
     def split_block(s, ch, b):
         x = vw[s, ch, b]
         hi = x.astype(BF16)
-        vhl[b, :R, :] = hi
-        vhl[b, R:, :] = (x - hi.astype(F32)).astype(BF16)
+        vhl[b, pl.ds(ch * R, R), :] = hi
+        vhl[b, pl.ds((CH + ch) * R, R), :] = (x - hi.astype(F32)).astype(BF16)
 
     def recv_ag(s, ch):
         @pl.loop(0, NB)
@@ -198,23 +198,28 @@
             def _(b, p=p):
                 split_block(s, ch, other + p * PB + b)
 
-    def product(rows, c, m):
-        lhs = jnp.concatenate([vhl[rows[j, c]] for j in range(3)], axis=1)
+    def product(lhs, m, c):
+        n = lhs.shape[0] // 2
         a = jnp.dot(lhs, whi[m, c], preferred_element_type=F32)
-        b = jnp.dot(lhs[:R], wlo[m, c], preferred_element_type=F32)
-        return a[:R] + a[R:] + b
+        b = jnp.dot(lhs[:n], wlo[m, c], preferred_element_type=F32)
+        return a[:n] + a[n:] + b
 
     def kill(s, ch, p):
         @pl.loop(p * PB, (p + 1) * PB)
         def _(c):
-            kb[s, ch, c] = product(krows, c, 1)
+            part = lambda at: jnp.concatenate(
+                [vhl[krows[j, c], pl.ds(at * R, R), :] for j in range(3)], axis=1
+            )
+            kb[s, ch, c] = product(jnp.concatenate([part(ch), part(CH + ch)], axis=0), 1, c)
 
         send_k(s, ch, p)
 
-    def queue(ch):
+    def queue():
         @pl.loop(0, NB)
         def _(c):
-            qb[ch, c] = product(qrows, c, 0)
+            both = product(jnp.concatenate([vhl[qrows[j, c]] for j in range(3)], axis=1), 0, c)
+            for ch in range(CH):
+                qb[ch, c] = both[ch * R : (ch + 1) * R]
 
     def forward(s, ch, p):
         if p < PIECES // 2:
@@ -317,23 +322,23 @@
             f(s, ch, p)
 
     weights(1)
+    weights(0)
     for s in range(STEPS):
         recv_ag(s, 0)
         all_of(kill, s, 0)
-        if s == 0:
-            weights(0)
-        queue(0)
         all_of(sums, s, 0, early)
         all_of(forward, s, 0, late)
         recv_ag(s, 1)
         all_of(kill, s, 1)
         all_of(sums, s, 0, late)
         all_of(forward, s, 0, early)
-        queue(1)
+        queue()
+        all_of(forward, s, 1, late)
         for p in every:
             comb(s, 0, p)
-            sums(s, 1, p)
-        all_of(forward, s, 1, late)
+            if p >= 2:
+                sums(s, 1, p - 2)
+        all_of(sums, s, 1, late)
         all_of(forward, s, 1, early)
         all_of(comb, s, 1)
 
@@ -368,7 +373,7 @@
         out_specs=pl.BlockSpec(memory_space=pl.ANY),
         scratch_shapes=[
             buf(STEPS, CH, 2 * NB, R, BS),
-            pltpu.VMEM((2 * NB, 2 * R, BS), BF16),
+            pltpu.VMEM((2 * NB, 2 * CH * R, BS), BF16),
             buf(*full),
             buf(CH, NB, R, BS),
             buf(*full), buf(*full),

time: 57.5 us -> 56.6 us (0.984); the launches traced: 56.7 us -> 56.4 us
  no operation moved by 1% of the time
where the time goes in v3:
time: 56.6 us; the launch traced here: 56.4 us
  Pallas kernels  54.5 us (96%)
  local copies, waits for them, and re-layouts  1.87 us (3%)
    pallas_call x1, Pallas kernels, local(): pl.pallas_call(kernel, out_shape=jax.ShapeDtypeStruct(state.shape, F32),...  54.5 us
    unnamed x1, local copies, waits for them, and re-layouts  1.87 us

profile of v3, /device:TPU:68, one launch (start us, length us, event | category | flops | bytes accessed | tf_op | source)
XLA Modules:
  0.0 56.4 jit_solution(11383844798191510253)
XLA Ops:
  0.0 54.5 %chain.1 = f32[64,2048]{1,0:T(8,128)} custom-call(f32[64,2048]{1,0:T(8,128)} %st.1, f32[8,768,256]{2,1,0:T(8,128)} %bitcast.5, f32[8,768,256]{2,1,0:T(8,128)} %bitcast.6, s32[3,8]{1,0:T(4,128)} %bitcast.7, s32[3,8]{1,0:T(4,128)} %bitcast.8, s32[12]{0:T(128)} %rindex.1, f32[2,8]{1,0:T(2,128)} %bitcast.9), custom_call_target="tpu_custom_call" | custom-call | tf_op jit(solution)/shard_map/chain/pallas_call | solution.py:368
  54.5 1.9 %copy.9 = f32[64,2048]{1,0:T(8,128)} copy(f32[64,2048]{1,0:T(8,128)} %chain.1) | data formatting | bytes 1048576

commit v4 on v3

--- a/solution.py
+++ b/solution.py
@@ -14,9 +14,10 @@
 R = 32
 NB = 8
 BS = 256
-PIECES = 4
+PIECES = 8
 PB = NB // PIECES
 SLOTS = 2 * NB
+LAG = 4
 KINDS = 8
 AG, YA, ZA, YB, ZB, CO, XF, XH = range(KINDS)
 MESH = pl.DeviceIdType.MESH
@@ -336,9 +337,9 @@
         all_of(forward, s, 1, late)
         for p in every:
             comb(s, 0, p)
-            if p >= 2:
-                sums(s, 1, p - 2)
-        all_of(sums, s, 1, late)
+            if p >= LAG:
+                sums(s, 1, p - LAG)
+        all_of(sums, s, 1, every[-LAG:])
         all_of(forward, s, 1, early)
         all_of(comb, s, 1)
 

time: 56.6 us -> 59.5 us (1.051); the launches traced: 56.4 us -> 58.5 us
  Pallas kernels: 54.5 us -> 56.6 us
    pallas_call x1, Pallas kernels: 54.5 us -> 56.6 us  [local(): pl.pallas_call(kernel, out_shape=jax.ShapeDtypeStruct(state.shape, F32),...]
where the time goes in v4:
time: 59.5 us; the launch traced here: 58.5 us
  Pallas kernels  56.6 us (95%)
  local copies, waits for them, and re-layouts  1.87 us (3%)
    pallas_call x1, Pallas kernels, local(): pl.pallas_call(kernel, out_shape=jax.ShapeDtypeStruct(state.shape, F32),...  56.6 us
    unnamed x1, local copies, waits for them, and re-layouts  1.87 us

profile of v4, /device:TPU:68, one launch (start us, length us, event | category | flops | bytes accessed | tf_op | source)
XLA Modules:
  0.0 58.5 jit_solution(3144927673149933524)
XLA Ops:
  0.0 56.6 %chain.1 = f32[64,2048]{1,0:T(8,128)} custom-call(f32[64,2048]{1,0:T(8,128)} %st.1, f32[8,768,256]{2,1,0:T(8,128)} %bitcast.5, f32[8,768,256]{2,1,0:T(8,128)} %bitcast.6, s32[3,8]{1,0:T(4,128)} %bitcast.7, s32[3,8]{1,0:T(4,128)} %bitcast.8, s32[12]{0:T(128)} %rindex.1, f32[2,8]{1,0:T(2,128)} %bitcast.9), custom_call_target="tpu_custom_call" | custom-call | tf_op jit(solution)/shard_map/chain/pallas_call | solution.py:369
  56.6 1.9 %copy.9 = f32[64,2048]{1,0:T(8,128)} copy(f32[64,2048]{1,0:T(8,128)} %chain.1) | data formatting | bytes 1048576
